TPU v7x, 512 devices: a whole 4x4x16 slice. The times are simulated.
512 devices in a mesh: dp: 8 (over y, z_hi), seq: 64 (over x, z_lo, core).
Axes of the slice: x: 4, y: 4, z: 16 (z_hi: 2, z_lo: 8; z = z_hi * 8 + z_lo), core: 2. Of those that a mesh axis runs over, the one named last changes fastest.
Arguments:
- grad_out: bfloat16 [8, 2048, 8192], P('dp', None, 'seq'), may hold values from -6 to 6
- gate: bfloat16 [8, 2048, 8192], P('dp', None, 'seq'), may hold values from -6 to 6
- value: bfloat16 [8, 2048, 8192], P('dp', None, 'seq'), may hold values from -6 to 6
- filter_taps: bfloat16 [2048, 8192], P(None, 'seq'), may hold values from -2 to 2
Outputs:
- grad_gate: bfloat16 [8, 2048, 8192], P('dp', None, 'seq')
- grad_value: bfloat16 [8, 2048, 8192], P('dp', None, 'seq')
- grad_filter: float32 [2048, 8192], P('seq', 'dp')
All inputs are finite; a program needn't handle non-finite values.
Results may differ from a plain program's by a relative error of at most 0.017.
Values may be sent and summed in bfloat16 or wider, within the bound.
A program may use at most 128 MiB of HBM per device.

v0:
```python
import math

import jax
import jax.numpy as jnp
from jax import lax
from jax.sharding import PartitionSpec as P

two_pi = 6.283185307179586


def split_parts(array):
    high_part = array.astype(jnp.bfloat16)
    low_part = (array - high_part.astype(jnp.float32)).astype(jnp.bfloat16)
    return (high_part, low_part)


def split_dot(left, right):
    left_high, left_low = split_parts(left)
    right_high, right_low = split_parts(right)
    wide_left = jnp.concatenate([left_high, left_high, left_low], 1)
    tall_right = jnp.concatenate([right_high, right_low, right_high], 0)
    return jnp.dot(wide_left, tall_right, preferred_element_type=jnp.float32)


def table_dot(table, signal):
    table_high, table_low = split_parts(table)
    wide_table = jnp.concatenate([table_high, table_low], 1)
    tall_signal = jnp.concatenate([signal, signal], 0)
    return jnp.dot(wide_table, tall_signal, preferred_element_type=jnp.float32)


def angle_table(rows, cols, period):
    row_idx = lax.broadcasted_iota(jnp.int32, (rows, cols), 0)
    col_idx = lax.broadcasted_iota(jnp.int32, (rows, cols), 1)
    return two_pi / period * (row_idx * col_idx % period).astype(jnp.float32)


def make_tables(blocks, width):
    outer = 2 * blocks
    total = outer * width
    start_angle = angle_table(outer, blocks, outer)
    start_table = jnp.concatenate([jnp.cos(start_angle), -jnp.sin(start_angle)], 0)
    twist = angle_table(outer, width, total)[:, None, :]
    inner = angle_table(width, width, width)
    finish_angle = angle_table(blocks, outer, outer)
    finish_table = jnp.concatenate([jnp.cos(finish_angle), -jnp.sin(finish_angle)], 1)
    return (
        start_table,
        jnp.cos(twist),
        jnp.sin(twist),
        jnp.cos(inner),
        jnp.sin(inner),
        finish_table,
    )


def complex_right(real_part, imag_part, table_cos, table_diff, table_sum):
    first = split_dot(real_part + imag_part, table_cos)
    second = split_dot(real_part, table_diff)
    third = split_dot(imag_part, table_sum)
    return (first - third, first + second)


def forward_spectrum(signal, tables):
    start_table, twist_cos, twist_sin, inner_cos, inner_sin, finish_table = tables
    blocks, group, width = signal.shape
    outer = 2 * blocks
    stacked = table_dot(start_table, signal.reshape(blocks, group * width))
    first_real = stacked[:outer].reshape(outer, group, width)
    first_imag = stacked[outer:].reshape(outer, group, width)
    turned_real = first_real * twist_cos + first_imag * twist_sin
    turned_imag = first_imag * twist_cos - first_real * twist_sin
    spec_real, spec_imag = complex_right(
        turned_real.reshape(outer * group, width),
        turned_imag.reshape(outer * group, width),
        inner_cos,
        -inner_sin - inner_cos,
        inner_cos - inner_sin,
    )
    return (spec_real.reshape(outer, group, width), spec_imag.reshape(outer, group, width))


def inverse_partial(spec_real, spec_imag, tables):
    start_table, twist_cos, twist_sin, inner_cos, inner_sin, finish_table = tables
    outer, group, width = spec_real.shape
    mid_real, mid_imag = complex_right(
        spec_real.reshape(outer * group, width),
        spec_imag.reshape(outer * group, width),
        inner_cos,
        inner_sin - inner_cos,
        inner_cos + inner_sin,
    )
    mid_real = mid_real.reshape(outer, group, width)
    mid_imag = mid_imag.reshape(outer, group, width)
    back_real = mid_real * twist_cos - mid_imag * twist_sin
    back_imag = mid_real * twist_sin + mid_imag * twist_cos
    return jnp.concatenate([back_real, back_imag], 0).reshape(2 * outer, group * width)


def inverse_signal(spec_real, spec_imag, tables):
    outer, group, width = spec_real.shape
    stacked = inverse_partial(spec_real, spec_imag, tables)
    signal = split_dot(tables[5], stacked) * (1.0 / (outer * width))
    return signal.reshape(outer // 2, group, width)


def spectral_product(left, right, conjugate):
    left_real, left_imag = left
    right_real, right_imag = right
    if conjugate:
        left_imag = -left_imag
    return (
        left_real * right_real - left_imag * right_imag,
        left_real * right_imag + left_imag * right_real,
    )


def on_device(grad_out, gate, value, filter_taps):
    nseq = lax.axis_size("seq")
    ndp = lax.axis_size("dp")
    chans = grad_out.shape[1]
    width = grad_out.shape[2]
    group = chans // nseq
    gated = (grad_out[0].astype(jnp.float32) * gate[0].astype(jnp.float32)).astype(jnp.bfloat16)
    gated = gated.reshape(nseq, group, width)
    values = value[0].reshape(nseq, group, width)
    gated_cols, value_cols, filter_cols = (
        lax.all_to_all(gated, "seq", split_axis=0, concat_axis=0, tiled=True),
        lax.all_to_all(values, "seq", split_axis=0, concat_axis=0, tiled=True),
        lax.all_to_all(
            filter_taps.reshape(nseq, group, width), "seq", split_axis=0, concat_axis=0, tiled=True
        ),
    )
    tables = make_tables(nseq, width)
    spec_gated = forward_spectrum(gated_cols, tables)
    spec_value = forward_spectrum(value_cols, tables)
    spec_filter = forward_spectrum(filter_cols, tables)
    conv_real, conv_imag = spectral_product(spec_filter, spec_value, False)
    conv = inverse_signal(conv_real, conv_imag, tables).astype(jnp.bfloat16)
    adj_real, adj_imag = spectral_product(spec_filter, spec_gated, True)
    value_grad = inverse_signal(adj_real, adj_imag, tables).astype(jnp.bfloat16)
    back_grad, back_conv = (
        lax.all_to_all(value_grad, "seq", split_axis=0, concat_axis=0, tiled=True),
        lax.all_to_all(conv, "seq", split_axis=0, concat_axis=0, tiled=True),
    )
    grad_gate = (
        grad_out[0].astype(jnp.float32) * back_conv.reshape(chans, width).astype(jnp.float32)
    ).astype(jnp.bfloat16)
    grad_value = back_grad.reshape(chans, width)
    cross_real, cross_imag = spectral_product(spec_value, spec_gated, True)
    cross_stack = inverse_partial(cross_real, cross_imag, tables)
    factor = 1.0 / (2 * nseq * width * ndp * math.sqrt(nseq * width))
    rows = nseq * width // ndp
    blocks_here = rows * lax.axis_size("dp") // width
    table = tables[5]
    taps = split_dot(table, cross_stack) * factor
    summed = lax.psum_scatter(
        taps.reshape(blocks_here, group, width)
        .transpose(0, 2, 1)
        .reshape(rows * lax.axis_size("dp"), group),
        "dp",
        scatter_dimension=0,
        tiled=True,
    )
    return (grad_gate[None], grad_value[None], summed.T)


def solution(mesh):
    return jax.shard_map(
        on_device,
        mesh=mesh,
        in_specs=(P("dp", None, "seq"), P("dp", None, "seq"), P("dp", None, "seq"), P(None, "seq")),
        out_specs=(P("dp", None, "seq"), P("dp", None, "seq"), P("seq", "dp")),
        check_vma=False,
    )
```

profile of v0, /device:TPU:1, one launch (start us, length us, event | category | flops | bytes accessed | tf_op | source)
XLA Modules:
  0.0 410.8 jit_solution(1810230515313775562)
XLA Ops:
  8.5 46.3 %all_to_all.25 = bf16[64,32,128]{2,1,0:T(8,128)(2,1)S(1)} all-to-all(bf16[64,32,128]{2,1,0:T(8,128)(2,1)S(1)} %bitcast.134), channel_id=1, replica_groups=mesh['dp'=8,'seq'=64] {'seq'}, dimensions={0} | all-to-all | bytes 1048576 | tf_op jit(solution)/shard_map/all_to_all | solution.py:128
  54.8 7.6 %all-to-all-start = ((bf16[64,32,128]{2,1,0:T(8,128)(2,1)}), bf16[64,32,128]{2,1,0:T(8,128)(2,1)S(1)}, u32[]{:S(2)}, u32[]{:S(2)}) async-start(bf16[64,32,128]{2,1,0:T(8,128)(2,1)} %bitcast), calls=%async_computation | async-start | bytes 1048576 | tf_op jit(solution)/shard_map/all_to_all | solution.py:130
  67.3 2.7 fusion.163
  70.1 21.8 %all-to-all-done = bf16[64,32,128]{2,1,0:T(8,128)(2,1)S(1)} async-done(((bf16[64,32,128]{2,1,0:T(8,128)(2,1)}), bf16[64,32,128]{2,1,0:T(8,128)(2,1)S(1)}, u32[]{:S(2)}, u32[]{:S(2)}) %all-to-all-start) | async-done | bytes 524320 | tf_op jit(solution)/shard_map/all_to_all | solution.py:130
  91.9 8.2 %all-to-all-start.1 = ((bf16[64,32,128]{2,1,0:T(8,128)(2,1)}), bf16[64,32,128]{2,1,0:T(8,128)(2,1)S(1)}, u32[]{:S(2)}, u32[]{:S(2)}) async-start(bf16[64,32,128]{2,1,0:T(8,128)(2,1)} %bitcast.3), calls=%async_computation.1 | async-start | bytes 1048576 | tf_op jit(solution)/shard_map/all_to_all | solution.py:129
  100.1 4.7 %fusion.236 = (f32[128,4096]{1,0:T(8,128)}, f32[128,4096]{1,0:T(8,128)}) fusion(f32[256,4096]{1,0:T(8,128)} %fusion.163), kind=kLoop, calls=%fused_computation.323 | loop fusion | bytes 8388608 | tf_op jit(solution)/shard_map/slice | solution.py:69
  106.5 2.7 reshape.198
  112.5 2.8 reshape.189
  115.3 2.7 reshape.190
  118.0 11.5 %all-to-all-done.1 = bf16[64,32,128]{2,1,0:T(8,128)(2,1)S(1)} async-done(((bf16[64,32,128]{2,1,0:T(8,128)(2,1)}), bf16[64,32,128]{2,1,0:T(8,128)(2,1)S(1)}, u32[]{:S(2)}, u32[]{:S(2)}) %all-to-all-start.1) | async-done | bytes 524320 | tf_op jit(solution)/shard_map/all_to_all | solution.py:129
  132.8 2.8 reshape.192
  135.5 2.7 reshape.193
  138.2 8.7 %subtract_convert_fusion.10 = (bf16[4096,128]{1,0:T(8,128)(2,1)S(1)}, bf16[4096,128]{1,0:T(8,128)(2,1)S(1)}, f32[4096,128]{1,0:T(8,128)S(1)}, bf16[4096,128]{1,0...) fusion(f32[4096,128]{1,0:T(8,128)S(1)} %reshape.197, ...), kind=kLoop, calls=%fused_computation.187 | loop fusion | flops 22020096 | bytes 37879808 | tf_op jit(solution)/shard_map/convert_element_type | solution.py:13
  154.7 2.5 convolution_subtract_fusion.4
  157.2 2.5 convolution_add_fusion.5
  159.7 2.5 convolution_add_fusion.4
  164.7 10.5 %subtract_convert_fusion.4 = (bf16[4096,128]{0,1:T(8,128)(2,1)}, bf16[4096,128]{0,1:T(8,128)(2,1)}, f32[4096,128]{0,1:T(8,128)S(1)}, bf16[4096,128]{0,1:T(8,128)...) fusion(f32[4096,128]{0,1:T(8,128)} %convolution_add_fusion.4, ...), kind=kOutput, calls=%fused_computation.177 | convolution fusion | flops 435978240 | bytes 39911424 | tf_op jit(solution)/shard_map/dot_general | solution.py:22
  180.5 3.0 reshape.194
  183.6 4.7 %convolution_add_fusion.3 = f32[4096,128]{1,0:T(8,128)} fusion(f32[4096,128]{1,0:T(8,128)} %copy-done.34, bf16[4096,128]{0,1:T(8,128)(2,1)S(1)} %copy-done.23, bf16[4096,128]{0,1:T(8,128)(2,1)} %get-tuple-element.70, bf16[128,128]{1,0:T(8,128)(2,1)S(1)} %copy-done.26, bf16[128,128]{1,0:T(8,128)(2,1)S(1)} %copy-done.25), kind=kOutput, calls=%fused_computation.36 | convolution fusion | flops 412909568 | bytes 6356992 | tf_op jit(solution)/shard_map/dot_general | solution.py:22
  188.2 2.8 reshape.195
  191.0 2.6 add_convert_fusion.1
  198.5 2.9 reshape.199
  201.4 4.7 %convolution_add_fusion.1 = f32[4096,128]{1,0:T(8,128)} fusion(f32[4096,128]{1,0:T(8,128)} %copy-done.35, bf16[4096,128]{0,1:T(8,128)(2,1)S(1)} %copy-done.12, bf16[4096,128]{0,1:T(8,128)(2,1)} %get-tuple-element.76, bf16[128,128]{1,0:T(8,128)(2,1)S(1)} %copy-done.26, bf16[128,128]{1,0:T(8,128)(2,1)S(1)} %copy-done.25), kind=kOutput, calls=%fused_computation.32 | convolution fusion | flops 412909568 | bytes 6356992 | tf_op jit(solution)/shard_map/dot_general | solution.py:22
  206.1 2.8 reshape.200
  215.9 3.3 convolution_add_fusion
  223.1 10.0 %fusion.142 = (f32[128,4096]{1,0:T(8,128)S(1)}, f32[128,4096]{1,0:T(8,128)}, f32[128,4096]{1,0:T(8,128)S(1)}, f32[128,4096]{1,0:T(8,128)S(1)}, f32[128,4096]{1,0:T(8,128)}, /*index=5*/f32[128,4096]{1,0:T(8,128)}) fusion(f32[128,4096]{1,0:T(8,128)} %reshape.202, f32[128,4096]{1,0:T(8,128)} %reshape.201, f32[16,8,32,128]{3,2,1,0:T(8,128)S(1)} %bitcast.127, ...), kind=kLoop, calls=%fused_computation.168 | loop fusion | flops 9437184 | bytes 29360128 | tf_op jit(solution)/shard_map/sub | solution.py:95
  236.0 7.6 %all-to-all-start.4 = ((bf16[64,32,128]{2,1,0:T(8,128)(2,1)}), bf16[64,32,128]{2,1,0:T(8,128)(2,1)S(1)}, u32[]{:S(2)}, u32[]{:S(2)}) async-start(bf16[64,32,128]{2,1,0:T(8,128)(2,1)} %bitcast.25), calls=%async_computation.4 | async-start | bytes 1048576 | tf_op jit(solution)/shard_map/all_to_all | solution.py:143
  243.6 2.7 subtract_convert_fusion.2
  251.3 21.8 %all-to-all-done.4 = bf16[64,32,128]{2,1,0:T(8,128)(2,1)S(1)} async-done(((bf16[64,32,128]{2,1,0:T(8,128)(2,1)}), bf16[64,32,128]{2,1,0:T(8,128)(2,1)S(1)}, u32[]{:S(2)}, u32[]{:S(2)}) %all-to-all-start.4) | async-done | bytes 524320 | tf_op jit(solution)/shard_map/all_to_all | solution.py:143
  273.0 7.6 %all-to-all-start.2 = ((bf16[64,32,128]{2,1,0:T(8,128)(2,1)}), bf16[64,32,128]{2,1,0:T(8,128)(2,1)S(1)}, u32[]{:S(2)}, u32[]{:S(2)}) async-start(bf16[64,32,128]{2,1,0:T(8,128)(2,1)} %bitcast.138), calls=%async_computation.2 | async-start | bytes 1048576 | tf_op jit(solution)/shard_map/all_to_all | solution.py:144
  285.4 24.7 %all-to-all-done.2 = bf16[64,32,128]{2,1,0:T(8,128)(2,1)S(1)} async-done(((bf16[64,32,128]{2,1,0:T(8,128)(2,1)}), bf16[64,32,128]{2,1,0:T(8,128)(2,1)S(1)}, u32[]{:S(2)}, u32[]{:S(2)}) %all-to-all-start.2) | async-done | bytes 524320 | tf_op jit(solution)/shard_map/all_to_all | solution.py:144
  311.0 91.8 %reduce-scatter.2.cloned.1.call-done = f32[1024,32]{0,1:T(8,128)} async-done(((f32[8192,32]{0,1:T(8,128)}), f32[1024,32]{0,1:T(8,128)}) %reduce-scatter.2.cloned.1.call-update) | async-done | bytes 131088 | tf_op jit(solution)/shard_map/reduce_scatter | solution.py:157
  (129 shorter events, 59.9 us)
Async XLA Ops:
  54.8 37.1 %all-to-all-start = ((bf16[64,32,128]{2,1,0:T(8,128)(2,1)}), bf16[64,32,128]{2,1,0:T(8,128)(2,1)S(1)}, u32[]{:S(2)}, u32[]{:S(2)}) async-start(bf16[64,32,128]{2,1,0:T(8,128)(2,1)} %bitcast), calls=%async_computation | async-start | bytes 1048576 | tf_op jit(solution)/shard_map/all_to_all | solution.py:130
  91.9 37.6 %all-to-all-start.1 = ((bf16[64,32,128]{2,1,0:T(8,128)(2,1)}), bf16[64,32,128]{2,1,0:T(8,128)(2,1)S(1)}, u32[]{:S(2)}, u32[]{:S(2)}) async-start(bf16[64,32,128]{2,1,0:T(8,128)(2,1)} %bitcast.3), calls=%async_computation.1 | async-start | bytes 1048576 | tf_op jit(solution)/shard_map/all_to_all | solution.py:129
  152.2 2.5 copy-start.19
  152.2 2.5 copy-start.20
  154.7 2.5 copy-start.17
  154.7 2.5 copy-start.18
  154.7 2.5 copy-start.31
  154.7 2.5 copy-start.32
  157.2 2.5 copy-start.13
  157.2 2.5 copy-start.14
  159.7 2.5 copy-start.10
  159.7 2.5 copy-start.11
  175.6 2.4 copy-start.24
  175.6 2.4 copy-start.29
  175.6 2.4 copy-start.30
  180.5 3.1 copy-start.23
  180.5 3.1 copy-start.25
  180.5 3.1 copy-start.26
  193.6 2.4 copy-start.15
  193.6 2.4 copy-start.16
  198.5 2.9 copy-start.12
  210.8 2.5 copy-start.8
  210.9 2.5 copy-start.9
  220.8 2.2 copy-start.4
  236.0 37.1 %all-to-all-start.4 = ((bf16[64,32,128]{2,1,0:T(8,128)(2,1)}), bf16[64,32,128]{2,1,0:T(8,128)(2,1)S(1)}, u32[]{:S(2)}, u32[]{:S(2)}) async-start(bf16[64,32,128]{2,1,0:T(8,128)(2,1)} %bitcast.25), calls=%async_computation.4 | async-start | bytes 1048576 | tf_op jit(solution)/shard_map/all_to_all | solution.py:143
  243.5 2.9 copy-start.1
  243.5 3.5 copy-start.2
  247.3 2.3 copy-start
  273.0 37.1 %all-to-all-start.2 = ((bf16[64,32,128]{2,1,0:T(8,128)(2,1)}), bf16[64,32,128]{2,1,0:T(8,128)(2,1)S(1)}, u32[]{:S(2)}, u32[]{:S(2)}) async-start(bf16[64,32,128]{2,1,0:T(8,128)(2,1)} %bitcast.138), calls=%async_computation.2 | async-start | bytes 1048576 | tf_op jit(solution)/shard_map/all_to_all | solution.py:144
  280.6 122.2 %reduce-scatter.2.cloned.1.call-start = ((), (), s32[]{:S(2)}) async-start(), calls=%async_computation.6 | async-start | bytes 1179648 | tf_op jit(solution)/shard_map/reduce_scatter | solution.py:157
  280.6 2.2 copy-start.5
  284.3 25.8 %copy-start.6 = (bf16[1,2048,128]{2,1,0:T(8,128)(2,1)S(1)}, bf16[1,2048,128]{2,1,0:T(8,128)(2,1)}, u32[]{:S(2)}) copy-start(bf16[1,2048,128]{2,1,0:T(8,128)(2,1)} %param.4) | copy-start | bytes 1572868
  (9 other events, 11.6 us)
Sparse Core Ops, SparseCore 0:
  286.5 116.3 reduce-scatter.1
where the time goes:
time: 417 us; the launch traced here: 411 us
  waiting for transfers between devices  172 us (41%)
  matrix products  56.2 us (13%)
  local copies, waits for them, and re-layouts  52.2 us (13%)
  blocking collectives  46.3 us (11%)
  other arithmetic  38.8 us (9%)
  starting transfers between devices  30.9 us (7%)
  between operations  14.8 us (4%)
    reduce_scatter x1, waiting for transfers between devices, on_device(): lax.psum_scatter(taps.reshape(blocks_here, group, width).transpose(0, 2,...  91.8 us
    dot_general x21, matrix products, split_dot(): return jnp.dot(wide_left, tall_right, preferred_element_type=jnp.float32)  51.9 us
    all_to_all x1, blocking collectives, on_device(): lax.all_to_all(gated, 'seq', split_axis=0, concat_axis=0, tiled=True)  46.3 us
    all_to_all x1, waiting for transfers between devices, on_device(): lax.all_to_all(conv, 'seq', split_axis=0, concat_axis=0, tiled=True)  24.7 us
    all_to_all x1, waiting for transfers between devices, on_device(): lax.all_to_all(filter_taps.reshape(nseq, group, width), 'seq', split_axis...  21.8 us
    all_to_all x1, waiting for transfers between devices, on_device(): lax.all_to_all(value_grad, 'seq', split_axis=0, concat_axis=0, tiled=True)  21.8 us
    convert_element_type x11, other arithmetic, split_parts(): low_part = (array - high_part.astype(jnp.float32)).astype(jnp.bfloat16)  17.3 us
    all_to_all x1, waiting for transfers between devices, on_device(): lax.all_to_all(values, 'seq', split_axis=0, concat_axis=0, tiled=True)  11.5 us
  transfers between devices with their start and end apart: 5, of which 5 were waited for; matrix products, arithmetic and copies ran while one was open for 9% of the time, Pallas kernels for 0%

commit v1 on v0

v1 whole, which is shorter than its diff:
```python
import functools
import math

import jax
import jax.numpy as jnp
import numpy as np
from jax import lax
from jax.experimental import pallas as pl
from jax.experimental.pallas import tpu as pltpu
from jax.sharding import PartitionSpec as P

MESH = pl.DeviceIdType.MESH
GROUP = 16


def make_tables(blocks, width, offset=0.25):
    total = blocks * width
    source = np.arange(blocks)
    lane = np.arange(width)
    start_angle = 2 * np.pi * ((source[:, None] + offset) * source[None, :] % blocks) / blocks
    start = np.concatenate([np.cos(start_angle), -np.sin(start_angle)], 0)
    twist = 2 * np.pi * ((source[:, None] + offset) * lane[None, :] % total) / total
    inner = 2 * np.pi * (lane[:, None] * lane[None, :] % width) / width
    cos, sin = np.cos(inner), np.sin(inner)
    forward = np.block([[cos, -sin], [sin, cos]])
    backward = np.block([[cos, sin], [-sin, cos]])
    finish = np.concatenate([np.cos(start_angle.T), -np.sin(start_angle.T)], 1) / total
    narrow = [jnp.asarray(table, jnp.bfloat16) for table in (start, forward, backward, finish)]
    wide = [jnp.asarray(table, jnp.float32) for table in (np.cos(twist), np.sin(twist))]
    return (*narrow, *wide)


def dot(left, right):
    return jnp.dot(left, right, preferred_element_type=jnp.float32)


def forward_spectrum(signal, spectrum, mixed, tables):
    start, forward, _, _, twist_cos, twist_sin = tables
    blocks, chans, width = signal.shape

    def body(step, carry):
        first = pl.multiple_of(step * GROUP, GROUP)
        columns = signal[:, pl.ds(first, GROUP), :].astype(jnp.float32)
        columns = jnp.swapaxes(columns, 0, 1).astype(jnp.bfloat16)
        cos, sin = twist_cos[...], twist_sin[...]
        for chan in range(GROUP):
            stage = dot(start[...], columns[chan])
            real, imag = stage[:blocks], stage[blocks:]
            rows = slice(chan * blocks, (chan + 1) * blocks)
            mixed[rows, :width] = (real * cos + imag * sin).astype(jnp.bfloat16)
            mixed[rows, width:] = (imag * cos - real * sin).astype(jnp.bfloat16)
        spectrum[pl.ds(first * blocks, GROUP * blocks), :] = dot(mixed[...], forward[...])
        return carry

    lax.fori_loop(0, chans // GROUP, body, 0)


def inverse_product(left, right, conjugate, result, mixed, partial, columns, tables):
    _, _, backward, finish, twist_cos, twist_sin = tables
    blocks, chans, width = result.shape

    def body(step, carry):
        first = pl.multiple_of(step * GROUP, GROUP)
        rows = pl.ds(first * blocks, GROUP * blocks)
        left_real, left_imag = left[rows, :width], left[rows, width:]
        right_real, right_imag = right[rows, :width], right[rows, width:]
        if conjugate:
            real = left_real * right_real + left_imag * right_imag
            imag = left_real * right_imag - left_imag * right_real
        else:
            real = left_real * right_real - left_imag * right_imag
            imag = left_real * right_imag + left_imag * right_real
        mixed[:, :width] = real.astype(jnp.bfloat16)
        mixed[:, width:] = imag.astype(jnp.bfloat16)
        partial[...] = dot(mixed[...], backward[...])
        cos, sin = twist_cos[...], twist_sin[...]
        for chan in range(GROUP):
            here = slice(chan * blocks, (chan + 1) * blocks)
            real, imag = partial[here, :width], partial[here, width:]
            turned = jnp.concatenate([real * cos - imag * sin, real * sin + imag * cos], 0)
            columns[chan] = dot(finish[...], turned.astype(jnp.bfloat16))
        result[:, pl.ds(first, GROUP), :] = jnp.swapaxes(columns[...], 0, 1).astype(result.dtype)
        return carry

    lax.fori_loop(0, chans // GROUP, body, 0)


def scatter(source, target, send_sem, recv_sem, me, nseq):
    def body(shift, carry):
        peer = lax.rem(me + shift, nseq)
        pltpu.make_async_remote_copy(
            src_ref=source.at[peer],
            dst_ref=target.at[me],
            send_sem=send_sem,
            recv_sem=recv_sem,
            device_id={"seq": peer},
            device_id_type=MESH,
        ).start()
        return carry

    lax.fori_loop(1, nseq, body, 0)
    pltpu.make_async_copy(source.at[me], target.at[me], recv_sem).start()


def take(ref, sem):
    pltpu.make_async_copy(ref, ref, sem).wait()


def kernel(
    factor,
    value,
    gated,
    taps,
    start,
    forward,
    backward,
    finish,
    twist_cos,
    twist_sin,
    conv_back,
    grad_back,
    filter_grad,
    value_cols,
    gated_cols,
    taps_cols,
    conv_send,
    grad_send,
    cross,
    y_recv,
    z_send,
    z_recv,
    spec_value,
    spec_gated,
    spec_taps,
    mixed,
    partial,
    columns,
    send_sem,
    recv_sem,
):
    tables = (start, forward, backward, finish, twist_cos, twist_sin)
    nseq = value.shape[0]
    me = lax.axis_index("seq")
    dp = lax.axis_index("dp")
    plane, half = dp // 2, lax.rem(dp, 2)
    depth = lax.rem(me // 2, 4)
    other_half = plane * 2 + 1 - half
    flat_taps = taps_cols

    barrier = pltpu.get_barrier_semaphore()

    def greet(shift, carry):
        pl.semaphore_signal(
            barrier, inc=1, device_id={"seq": lax.rem(me + shift, nseq)}, device_id_type=MESH
        )
        return carry

    lax.fori_loop(1, nseq, greet, 0)
    for shift in range(1, 4):
        neighbour = lax.rem(plane + shift, 4) * 2 + half
        pl.semaphore_signal(barrier, inc=1, device_id={"dp": neighbour}, device_id_type=MESH)
    pl.semaphore_signal(barrier, inc=1, device_id={"dp": other_half}, device_id_type=MESH)
    pl.semaphore_wait(barrier, nseq + 3)

    def quarter(depth_here):
        return lax.rem(plane + 4 - depth_here, 4)

    mine = quarter(depth)

    def send_taps(step, carry):
        peer = (step // 2) * 8 + mine * 2 + lax.rem(step, 2)

        @pl.when(peer != me)
        def _():
            pltpu.make_async_remote_copy(
                src_ref=taps.at[peer // 8, lax.rem(peer // 2, 4), lax.rem(peer, 2)],
                dst_ref=taps_cols.at[me // 8, depth, lax.rem(me, 2)],
                send_sem=send_sem.at[0],
                recv_sem=recv_sem.at[0],
                device_id={"seq": peer},
                device_id_type=MESH,
            ).start()

        @pl.when(peer == me)
        def _():
            pltpu.make_async_copy(
                taps.at[me // 8, depth, lax.rem(me, 2)],
                taps_cols.at[me // 8, depth, lax.rem(me, 2)],
                recv_sem.at[0],
            ).start()

        return carry

    lax.fori_loop(0, nseq // 4, send_taps, 0)
    scatter(value, value_cols, send_sem.at[1], recv_sem.at[1], me, nseq)
    scatter(gated, gated_cols, send_sem.at[2], recv_sem.at[2], me, nseq)

    take(taps_cols.at[:, mine], recv_sem.at[0])
    for shift in range(1, 4):
        neighbour = lax.rem(plane + shift, 4) * 2 + half
        pltpu.make_async_remote_copy(
            src_ref=taps_cols.at[:, mine],
            dst_ref=taps_cols.at[:, mine],
            send_sem=send_sem.at[3],
            recv_sem=recv_sem.at[3],
            device_id={"dp": neighbour},
            device_id_type=MESH,
        ).start()
    take(taps_cols.at[:, pl.ds(0, 3)], recv_sem.at[3])
    taps_view = taps_cols.reshape(value.shape)
    forward_spectrum(taps_view, spec_taps, mixed, tables)

    take(value_cols, recv_sem.at[1])
    forward_spectrum(value_cols, spec_value, mixed, tables)
    inverse_product(spec_taps, spec_value, False, conv_send, mixed, partial, columns, tables)
    scatter(conv_send, conv_back, send_sem.at[4], recv_sem.at[4], me, nseq)

    take(gated_cols, recv_sem.at[2])
    forward_spectrum(gated_cols, spec_gated, mixed, tables)
    inverse_product(spec_taps, spec_gated, True, grad_send, mixed, partial, columns, tables)
    scatter(grad_send, grad_back, send_sem.at[5], recv_sem.at[5], me, nseq)

    inverse_product(spec_value, spec_gated, True, cross, mixed, partial, columns, tables)
    for shift in range(1, 4):
        other = lax.rem(plane + shift, 4)
        pltpu.make_async_remote_copy(
            src_ref=cross.at[pl.ds(other * 16, 16)],
            dst_ref=y_recv.at[shift - 1],
            send_sem=send_sem.at[6],
            recv_sem=recv_sem.at[6],
            device_id={"dp": other * 2 + half},
            device_id_type=MESH,
        ).start()
    take(y_recv, recv_sem.at[6])
    gone = plane * 16 + 8 * (1 - half)
    away = pl.ds(8 * (1 - half), 8)
    z_send[...] = (
        cross[pl.ds(gone, 8)] + y_recv[0, away] + y_recv[1, away] + y_recv[2, away]
    ).astype(z_send.dtype)
    swap = pltpu.make_async_remote_copy(
        src_ref=z_send,
        dst_ref=z_recv,
        send_sem=send_sem.at[7],
        recv_sem=recv_sem.at[7],
        device_id={"dp": other_half},
        device_id_type=MESH,
    )
    swap.start()
    kept = plane * 16 + 8 * half
    stay = pl.ds(8 * half, 8)
    total = cross[pl.ds(kept, 8)] + y_recv[0, stay] + y_recv[1, stay] + y_recv[2, stay]
    swap.wait()
    width = value.shape[2]
    total = (total + z_recv[...].astype(jnp.float32)) * factor
    for block in range(8):
        filter_grad[:, block * width : (block + 1) * width] = total[block]

    take(conv_back, recv_sem.at[4])
    take(grad_back, recv_sem.at[5])
    for index, ref in ((1, value), (2, gated), (4, conv_send), (5, grad_send)):
        take(ref.at[pl.ds(0, nseq - 1)], send_sem.at[index])
    take(taps_cols.at[:, pl.ds(0, 3)], send_sem.at[3])
    take(y_recv, send_sem.at[6])

    @pl.when(mine == depth)
    def _():
        take(value.at[pl.ds(0, nseq // 4 - 1)], send_sem.at[0])

    @pl.when(mine != depth)
    def _():
        take(value.at[pl.ds(0, nseq // 4)], send_sem.at[0])


def run_kernel(value, gated, taps, factor):
    nseq, group, width = value.shape
    narrow, wide = jnp.bfloat16, jnp.float32
    blocks = (nseq, group, width)
    shapes = [
        jax.ShapeDtypeStruct(blocks, narrow),
        jax.ShapeDtypeStruct(blocks, narrow),
        jax.ShapeDtypeStruct((group, nseq * width // 8), wide),
    ]
    tables = make_tables(nseq, width)
    quarters = (nseq // 8, 4, 2, group, width)
    spec = (group * nseq, 2 * width)
    part = (GROUP * nseq, 2 * width)
    place = pl.BlockSpec(memory_space=pltpu.VMEM)
    return pl.pallas_call(
        functools.partial(kernel, factor),
        out_shape=shapes,
        in_specs=[place] * (3 + len(tables)),
        out_specs=[place] * 3,
        scratch_shapes=[
            pltpu.VMEM(blocks, narrow),
            pltpu.VMEM(blocks, narrow),
            pltpu.VMEM(quarters, narrow),
            pltpu.VMEM(blocks, narrow),
            pltpu.VMEM(blocks, narrow),
            pltpu.VMEM(blocks, wide),
            pltpu.VMEM((3, 16, group, width), wide),
            pltpu.VMEM((8, group, width), narrow),
            pltpu.VMEM((8, group, width), narrow),
            pltpu.VMEM(spec, wide),
            pltpu.VMEM(spec, wide),
            pltpu.VMEM(spec, wide),
            pltpu.VMEM(part, narrow),
            pltpu.VMEM(part, wide),
            pltpu.VMEM((GROUP, nseq, width), wide),
            pltpu.SemaphoreType.DMA((8,)),
            pltpu.SemaphoreType.DMA((8,)),
        ],
        compiler_params=pltpu.CompilerParams(
            collective_id=0, has_side_effects=True, vmem_limit_bytes=48 * 2**20
        ),
    )(value, gated, taps.reshape(quarters), *tables)


def on_device(grad_out, gate, value, filter_taps):
    nseq = lax.axis_size("seq")
    ndp = lax.axis_size("dp")
    chans, width = grad_out.shape[1:]
    blocks = (nseq, chans // nseq, width)
    gated = (grad_out[0].astype(jnp.float32) * gate[0].astype(jnp.float32)).astype(jnp.bfloat16)
    factor = 1.0 / (ndp * math.sqrt(nseq * width))
    conv, grad_value, grad_filter = run_kernel(
        value[0].reshape(blocks), gated.reshape(blocks), filter_taps.reshape(blocks), factor
    )
    conv = conv.reshape(chans, width)
    grad_gate = (grad_out[0].astype(jnp.float32) * conv.astype(jnp.float32)).astype(jnp.bfloat16)
    return (grad_gate[None], grad_value.reshape(1, chans, width), grad_filter)


def solution(mesh):
    return jax.shard_map(
        on_device,
        mesh=mesh,
        in_specs=(P("dp", None, "seq"), P("dp", None, "seq"), P("dp", None, "seq"), P(None, "seq")),
        out_specs=(P("dp", None, "seq"), P("dp", None, "seq"), P("seq", "dp")),
        check_vma=False,
    )
```

time: 417 us -> 125 us (0.30); the launches traced: 411 us -> 125 us
  waiting for transfers between devices: 172 us -> 0 us
  Pallas kernels: 0 us -> 120 us
  matrix products: 56.2 us -> 0 us
  local copies, waits for them, and re-layouts: 52.2 us -> 1.52 us
  blocking collectives: 46.3 us -> 0 us
  other arithmetic: 38.8 us -> 2.36 us
  starting transfers between devices: 30.9 us -> 0 us
  between operations: 14.8 us -> 0.76 us
    pallas_call x0 -> x1, Pallas kernels: none -> 120 us  [run_kernel(): pl.pallas_call(functools.partial(kernel, factor), out_shape=shapes, in_sp...]
    reduce_scatter x1 -> x0, waiting for transfers between devices: 91.8 us -> none  [on_device(): lax.psum_scatter(taps.reshape(blocks_here, group, width).transpose(0, 2,...]
    all_to_all x4 -> x0, waiting for transfers between devices: 79.7 us -> none  [the longest x1 24.7 us: on_device(): lax.all_to_all(conv, 'seq', split_axis=0, concat_axis=0, tiled=True)]
    dot_general x24 -> x0, matrix products: 56.2 us -> none  [the longest x21 51.9 us: split_dot(): return jnp.dot(wide_left, tall_right, preferred_element_type=jnp.float32)]
    all_to_all x1 -> x0, blocking collectives: 46.3 us -> none  [on_device(): lax.all_to_all(gated, 'seq', split_axis=0, concat_axis=0, tiled=True)]
    reshape x13 -> x0, local copies, waits for them, and re-layouts: 31.2 us -> none  [the longest x3 8.19 us: forward_spectrum(): first_imag = stacked[outer:].reshape(outer, group, width)]
    all_to_all x4 -> x0, starting transfers between devices: 30.9 us -> none  [the longest x1 8.2 us: on_device(): lax.all_to_all(values, 'seq', split_axis=0, concat_axis=0, tiled=True)]
    convert_element_type x23 -> x1, other arithmetic: 26.7 us -> 0.93 us  [on_device(): (grad_out[0].astype(jnp.float32) * conv.astype(jnp.float32)).astype(jnp.b...]
  transfers between devices with their start and end apart: 5 -> 0, of which waited for: 5 -> 0; matrix products, arithmetic and copies ran while one was open for 9% -> 0% of each run, Pallas kernels for 0% -> 0%
where the time goes in v1:
time: 125 us
  Pallas kernels  120 us (96%)
  other arithmetic  2.36 us (2%)
  local copies, waits for them, and re-layouts  1.52 us (1%)
    pallas_call x1, Pallas kernels, run_kernel(): pl.pallas_call(functools.partial(kernel, factor), out_shape=shapes, in_sp...  120 us

profile of v1, /device:TPU:1, one launch (start us, length us, event | category | flops | bytes accessed | tf_op | source)
XLA Modules:
  0.0 124.8 jit_solution(7584098585041792556)
XLA Ops:
  0.6 0.0 copy-start
  0.6 0.0 copy-start.1
  0.7 0.0 copy-start.2
  0.7 0.0 copy-start.3
  0.7 0.0 copy-start.4
  0.7 0.0 copy-start.5
  0.7 0.0 copy-start.6
  0.7 0.0 copy-start.7
  0.7 1.4 %fusion = bf16[1,2048,128]{2,1,0:T(8,128)(2,1)S(1)} fusion(bf16[1,2048,128]{2,1,0:T(8,128)(2,1)} %param.10, bf16[1,2048,128]{2,1,0:T(8,128)(2,1)} %param.11), kind=kLoop, calls=%fused_computation.2 | loop fusion | flops 1048576 | bytes 1572864 | tf_op jit(solution)/shard_map/convert_element_type | solution.py:323
  2.2 0.0 copy-done
  2.2 0.0 copy-done.1
  2.2 0.0 copy-done.2
  2.2 0.0 copy-done.3
  2.2 0.0 copy-done.4
  2.2 0.0 copy-done.5
  2.2 0.0 copy-done.6
  2.2 0.0 copy-done.7
  2.2 0.0 copy-start.8
  2.2 120.2 %shard_map.121 = (bf16[64,32,128]{2,1,0:T(8,128)(2,1)S(1)}, bf16[64,32,128]{2,1,0:T(8,128)(2,1)S(1)}, f32[32,1024]{1,0:T(8,128)S(1)}) custom-call(bf16[64,32,128]{2,1,0:T(8,128)(2,1)S(1)} %bitcast.11, bf16[64,32,128]{2,1,0:T(8,128)(2,1)S(1)} %bitcast.8, bf16[8,4,2,32,128]{4,3,2,1,0:T(8,128)(2,1)S(1)} %bitcast.12, bf16[128,64]{1,0:T(8,128)(2,1)S(1)} %copy-done.6, ...), custom_call_target="tpu_custom_call" | custom-call | tf_op jit(solution)/shard_map/pallas_call | solution.py:288
  122.4 0.0 copy-done.8
  122.4 0.9 fusion.1
  123.4 0.8 copy.15
  124.2 0.7 copy.16
Async XLA Ops:
  0.6 1.5 %copy-start = (bf16[1,2048,128]{2,1,0:T(8,128)(2,1)S(1)}, bf16[1,2048,128]{2,1,0:T(8,128)(2,1)}, u32[]{:S(2)}) copy-start(bf16[1,2048,128]{2,1,0:T(8,128)(2,1)} %param.12) | copy-start | bytes 1572868
  0.6 1.5 %copy-start.1 = (bf16[2048,128]{1,0:T(8,128)(2,1)S(1)}, bf16[2048,128]{1,0:T(8,128)(2,1)}, u32[]{:S(2)}) copy-start(bf16[2048,128]{1,0:T(8,128)(2,1)} %param.13) | copy-start | bytes 1572868
  0.7 1.5 %copy-start.2 = (bf16[256,256]{1,0:T(8,128)(2,1)S(1)}, bf16[256,256]{1,0:T(8,128)(2,1)}, u32[]{:S(2)}) copy-start(bf16[256,256]{1,0:T(8,128)(2,1)} %constant.14.clone.backward) | copy-start | bytes 393220
  0.7 1.5 %copy-start.3 = (bf16[256,256]{1,0:T(8,128)(2,1)S(1)}, bf16[256,256]{1,0:T(8,128)(2,1)}, u32[]{:S(2)}) copy-start(bf16[256,256]{1,0:T(8,128)(2,1)} %constant.13.clone.forward) | copy-start | bytes 393220
  0.7 1.5 %copy-start.4 = (f32[64,128]{1,0:T(8,128)S(1)}, f32[64,128]{1,0:T(8,128)}, u32[]{:S(2)}) copy-start(f32[64,128]{1,0:T(8,128)} %constant.17.clone.twist_sin) | copy-start | bytes 98308
  0.7 1.5 %copy-start.5 = (f32[64,128]{1,0:T(8,128)S(1)}, f32[64,128]{1,0:T(8,128)}, u32[]{:S(2)}) copy-start(f32[64,128]{1,0:T(8,128)} %constant.16.clone.twist_cos) | copy-start | bytes 98308
  0.7 1.5 %copy-start.6 = (bf16[128,64]{1,0:T(8,128)(2,1)S(1)}, bf16[128,64]{1,0:T(8,128)(2,1)}, u32[]{:S(2)}) copy-start(bf16[128,64]{1,0:T(8,128)(2,1)} %constant.12.clone.start) | copy-start | bytes 49156
  0.7 1.5 %copy-start.7 = (bf16[64,128]{1,0:T(8,128)(2,1)S(1)}, bf16[64,128]{1,0:T(8,128)(2,1)}, u32[]{:S(2)}) copy-start(bf16[64,128]{1,0:T(8,128)(2,1)} %constant.15.clone.finish) | copy-start | bytes 49156
  2.2 120.2 %copy-start.8 = (bf16[1,2048,128]{2,1,0:T(8,128)(2,1)S(1)}, bf16[1,2048,128]{2,1,0:T(8,128)(2,1)}, u32[]{:S(2)}) copy-start(bf16[1,2048,128]{2,1,0:T(8,128)(2,1)} %param.10) | copy-start | bytes 1572868

commit v2 on v1

--- a/solution.py
+++ b/solution.py
@@ -11,6 +11,8 @@
 
 MESH = pl.DeviceIdType.MESH
 GROUP = 16
+EARLY = 40
+FIRST = 32
 
 
 def make_tables(blocks, width, offset=0.25):
@@ -85,7 +87,7 @@
     lax.fori_loop(0, chans // GROUP, body, 0)
 
 
-def scatter(source, target, send_sem, recv_sem, me, nseq):
+def scatter(source, target, send_sem, recv_sem, me, nseq, first=0, last=None):
     def body(shift, carry):
         peer = lax.rem(me + shift, nseq)
         pltpu.make_async_remote_copy(
@@ -98,18 +100,30 @@
         ).start()
         return carry
 
-    lax.fori_loop(1, nseq, body, 0)
-    pltpu.make_async_copy(source.at[me], target.at[me], recv_sem).start()
+    lax.fori_loop(max(first, 1), nseq if last is None else last, body, 0)
+    if first == 0:
+        pltpu.make_async_copy(source.at[me], target.at[me], recv_sem).start()
 
 
 def take(ref, sem):
     pltpu.make_async_copy(ref, ref, sem).wait()
 
 
+def times(left, right, result):
+    def body(step, carry):
+        rows = pl.ds(step * 8, 8)
+        product = left[rows].astype(jnp.float32) * right[rows].astype(jnp.float32)
+        result[rows] = product.astype(result.dtype)
+        return carry
+
+    lax.fori_loop(0, left.shape[0] // 8, body, 0)
+
+
 def kernel(
     factor,
+    grad_out,
+    gate,
     value,
-    gated,
     taps,
     start,
     forward,
@@ -117,15 +131,20 @@
     finish,
     twist_cos,
     twist_sin,
-    conv_back,
+    grad_gate,
     grad_back,
     filter_grad,
+    grad_held,
+    gate_held,
+    gated,
     value_cols,
     gated_cols,
     taps_cols,
     conv_send,
+    conv_back,
     grad_send,
     cross,
+    y_send,
     y_recv,
     z_send,
     z_recv,
@@ -135,8 +154,11 @@
     mixed,
     partial,
     columns,
+    gate_out,
+    filter_out,
     send_sem,
     recv_sem,
+    load_sem,
 ):
     tables = (start, forward, backward, finish, twist_cos, twist_sin)
     nseq = value.shape[0]
@@ -144,8 +166,14 @@
     dp = lax.axis_index("dp")
     plane, half = dp // 2, lax.rem(dp, 2)
     depth = lax.rem(me // 2, 4)
+    upper = lax.rem(me // 8, 2)
     other_half = plane * 2 + 1 - half
-    flat_taps = taps_cols
+    mine = lax.rem(plane + 4 - depth, 4)
+
+    def taps_peer(step):
+        far = lax.rem(step // 2, 2)
+        peer = (step // 2) * 8 + mine * 2 + lax.rem(step, 2)
+        return peer, plane * 2 + lax.rem(half + upper + far, 2)
 
     barrier = pltpu.get_barrier_semaphore()
 
@@ -155,33 +183,54 @@
         )
         return carry
 
+    def greet_taps(step, carry):
+        peer, row = taps_peer(step)
+
+        @pl.when(row != dp)
+        def _():
+            pl.semaphore_signal(
+                barrier, inc=1, device_id={"dp": row, "seq": peer}, device_id_type=MESH
+            )
+
+        return carry
+
     lax.fori_loop(1, nseq, greet, 0)
+    lax.fori_loop(0, nseq // 4, greet_taps, 0)
     for shift in range(1, 4):
         neighbour = lax.rem(plane + shift, 4) * 2 + half
         pl.semaphore_signal(barrier, inc=1, device_id={"dp": neighbour}, device_id_type=MESH)
     pl.semaphore_signal(barrier, inc=1, device_id={"dp": other_half}, device_id_type=MESH)
-    pl.semaphore_wait(barrier, nseq + 3)
-
-    def quarter(depth_here):
-        return lax.rem(plane + 4 - depth_here, 4)
-
-    mine = quarter(depth)
+
+    loads = [
+        pltpu.make_async_copy(grad_out, grad_held, load_sem.at[0]),
+        pltpu.make_async_copy(gate, gate_held, load_sem.at[1]),
+    ]
+    for load in loads:
+        load.start()
+    for load in loads:
+        load.wait()
+    times(grad_held, gate_held, gated)
+    pl.semaphore_wait(barrier, nseq + 3 + nseq // 8)
+
+    scatter(value, value_cols, send_sem.at[1], recv_sem.at[1], me, nseq, 0, EARLY)
+    scatter(value, value_cols, send_sem.at[1], recv_sem.at[8], me, nseq, EARLY)
 
     def send_taps(step, carry):
-        peer = (step // 2) * 8 + mine * 2 + lax.rem(step, 2)
-
-        @pl.when(peer != me)
+        peer, row = taps_peer(step)
+        itself = jnp.logical_and(peer == me, row == dp)
+
+        @pl.when(jnp.logical_not(itself))
         def _():
             pltpu.make_async_remote_copy(
                 src_ref=taps.at[peer // 8, lax.rem(peer // 2, 4), lax.rem(peer, 2)],
                 dst_ref=taps_cols.at[me // 8, depth, lax.rem(me, 2)],
                 send_sem=send_sem.at[0],
                 recv_sem=recv_sem.at[0],
-                device_id={"seq": peer},
+                device_id={"dp": row, "seq": peer},
                 device_id_type=MESH,
             ).start()
 
-        @pl.when(peer == me)
+        @pl.when(itself)
         def _():
             pltpu.make_async_copy(
                 taps.at[me // 8, depth, lax.rem(me, 2)],
@@ -192,7 +241,7 @@
         return carry
 
     lax.fori_loop(0, nseq // 4, send_taps, 0)
-    scatter(value, value_cols, send_sem.at[1], recv_sem.at[1], me, nseq)
+    take(value_cols.at[pl.ds(0, EARLY)], recv_sem.at[1])
     scatter(gated, gated_cols, send_sem.at[2], recv_sem.at[2], me, nseq)
 
     take(taps_cols.at[:, mine], recv_sem.at[0])
@@ -207,36 +256,41 @@
             device_id_type=MESH,
         ).start()
     take(taps_cols.at[:, pl.ds(0, 3)], recv_sem.at[3])
-    taps_view = taps_cols.reshape(value.shape)
-    forward_spectrum(taps_view, spec_taps, mixed, tables)
-
-    take(value_cols, recv_sem.at[1])
+    forward_spectrum(taps_cols.reshape(value.shape), spec_taps, mixed, tables)
+
+    take(value_cols.at[pl.ds(EARLY, nseq - EARLY)], recv_sem.at[8])
     forward_spectrum(value_cols, spec_value, mixed, tables)
     inverse_product(spec_taps, spec_value, False, conv_send, mixed, partial, columns, tables)
-    scatter(conv_send, conv_back, send_sem.at[4], recv_sem.at[4], me, nseq)
+    scatter(conv_send, conv_back, send_sem.at[4], recv_sem.at[4], me, nseq, 0, FIRST)
 
     take(gated_cols, recv_sem.at[2])
     forward_spectrum(gated_cols, spec_gated, mixed, tables)
-    inverse_product(spec_taps, spec_gated, True, grad_send, mixed, partial, columns, tables)
-    scatter(grad_send, grad_back, send_sem.at[5], recv_sem.at[5], me, nseq)
-
     inverse_product(spec_value, spec_gated, True, cross, mixed, partial, columns, tables)
     for shift in range(1, 4):
         other = lax.rem(plane + shift, 4)
+        y_send[shift - 1] = cross[pl.ds(other * 16, 16)].astype(y_send.dtype)
+    for shift in range(1, 4):
+        other = lax.rem(plane + shift, 4)
         pltpu.make_async_remote_copy(
-            src_ref=cross.at[pl.ds(other * 16, 16)],
+            src_ref=y_send.at[shift - 1],
             dst_ref=y_recv.at[shift - 1],
             send_sem=send_sem.at[6],
             recv_sem=recv_sem.at[6],
             device_id={"dp": other * 2 + half},
             device_id_type=MESH,
         ).start()
+    scatter(conv_send, conv_back, send_sem.at[4], recv_sem.at[4], me, nseq, FIRST)
+    inverse_product(spec_taps, spec_gated, True, grad_send, mixed, partial, columns, tables)
+    scatter(grad_send, grad_back, send_sem.at[5], recv_sem.at[5], me, nseq, 0, FIRST)
+
     take(y_recv, recv_sem.at[6])
-    gone = plane * 16 + 8 * (1 - half)
-    away = pl.ds(8 * (1 - half), 8)
-    z_send[...] = (
-        cross[pl.ds(gone, 8)] + y_recv[0, away] + y_recv[1, away] + y_recv[2, away]
-    ).astype(z_send.dtype)
+
+    def plane_sum(part):
+        rows = pl.ds(8 * part, 8)
+        terms = [y_recv[index, rows].astype(jnp.float32) for index in range(3)]
+        return cross[pl.ds(plane * 16 + 8 * part, 8)] + terms[0] + terms[1] + terms[2]
+
+    z_send[...] = plane_sum(1 - half).astype(z_send.dtype)
     swap = pltpu.make_async_remote_copy(
         src_ref=z_send,
         dst_ref=z_recv,
@@ -246,32 +300,71 @@
         device_id_type=MESH,
     )
     swap.start()
-    kept = plane * 16 + 8 * half
-    stay = pl.ds(8 * half, 8)
-    total = cross[pl.ds(kept, 8)] + y_recv[0, stay] + y_recv[1, stay] + y_recv[2, stay]
+    scatter(grad_send, grad_back, send_sem.at[5], recv_sem.at[5], me, nseq, FIRST)
+
+    take(conv_back, recv_sem.at[4])
+    times(grad_held, conv_back, gate_out)
+    gate_store = pltpu.make_async_copy(gate_out, grad_gate, load_sem.at[2])
+    gate_store.start()
+
+    total = plane_sum(half)
     swap.wait()
     width = value.shape[2]
     total = (total + z_recv[...].astype(jnp.float32)) * factor
     for block in range(8):
-        filter_grad[:, block * width : (block + 1) * width] = total[block]
-
-    take(conv_back, recv_sem.at[4])
-    take(grad_back, recv_sem.at[5])
-    for index, ref in ((1, value), (2, gated), (4, conv_send), (5, grad_send)):
+        filter_out[:, block * width : (block + 1) * width] = total[block]
+    filter_store = pltpu.make_async_copy(filter_out, filter_grad, load_sem.at[3])
+    filter_store.start()
+    gate_store.wait()
+
+    for index, ref in ((1, value_cols), (2, gated), (4, conv_send)):
         take(ref.at[pl.ds(0, nseq - 1)], send_sem.at[index])
     take(taps_cols.at[:, pl.ds(0, 3)], send_sem.at[3])
     take(y_recv, send_sem.at[6])
-
-    @pl.when(mine == depth)
+    itself_too = mine == depth
+
+    @pl.when(itself_too)
     def _():
-        take(value.at[pl.ds(0, nseq // 4 - 1)], send_sem.at[0])
-
-    @pl.when(mine != depth)
+        take(value_cols.at[pl.ds(0, nseq // 4 - 1)], send_sem.at[0])
+
+    @pl.when(jnp.logical_not(itself_too))
     def _():
-        take(value.at[pl.ds(0, nseq // 4)], send_sem.at[0])
-
-
-def run_kernel(value, gated, taps, factor):
+        take(value_cols.at[pl.ds(0, nseq // 4)], send_sem.at[0])
+
+    take(grad_send.at[pl.ds(0, nseq - 1)], send_sem.at[5])
+    filter_store.wait()
+    take(grad_back, recv_sem.at[5])
+
+
+def flush(*refs):
+    count = len(refs) // 3
+    sources, targets, held = refs[:count], refs[count : 2 * count], refs[2 * count : 3 * count]
+    loads, stores = [], []
+    for index in range(count):
+        rows = held[index].shape[0] // 4
+        for step in range(4):
+            part = pl.ds(step * rows, rows)
+            sem = 4 * index + step
+            loads.append(
+                pltpu.make_async_copy(
+                    sources[index].at[part], held[index].at[part], refs[-1].at[0, sem]
+                )
+            )
+            stores.append(
+                pltpu.make_async_copy(
+                    held[index].at[part], targets[index].at[part], refs[-1].at[1, sem]
+                )
+            )
+    for load in loads:
+        load.start()
+    for load, store in zip(loads, stores):
+        load.wait()
+        store.start()
+    for store in stores:
+        store.wait()
+
+
+def run_kernel(grad_out, gate, value, taps, factor):
     nseq, group, width = value.shape
     narrow, wide = jnp.bfloat16, jnp.float32
     blocks = (nseq, group, width)
@@ -285,19 +378,19 @@
     spec = (group * nseq, 2 * width)
     part = (GROUP * nseq, 2 * width)
     place = pl.BlockSpec(memory_space=pltpu.VMEM)
-    return pl.pallas_call(
+    far = pl.BlockSpec(memory_space=pl.ANY)
+    results = pl.pallas_call(
         functools.partial(kernel, factor),
         out_shape=shapes,
-        in_specs=[place] * (3 + len(tables)),
-        out_specs=[place] * 3,
-        scratch_shapes=[
-            pltpu.VMEM(blocks, narrow),
-            pltpu.VMEM(blocks, narrow),
-            pltpu.VMEM(quarters, narrow),
-            pltpu.VMEM(blocks, narrow),
-            pltpu.VMEM(blocks, narrow),
+        in_specs=[far] * 4 + [place] * len(tables),
+        out_specs=[far] * 3,
+        scratch_shapes=[pltpu.VMEM(blocks, narrow) for _ in range(5)]
+        + [pltpu.VMEM(quarters, narrow)]
+        + [pltpu.VMEM(blocks, narrow) for _ in range(3)]
+        + [
             pltpu.VMEM(blocks, wide),
-            pltpu.VMEM((3, 16, group, width), wide),
+            pltpu.VMEM((3, 16, group, width), narrow),
+            pltpu.VMEM((3, 16, group, width), narrow),
             pltpu.VMEM((8, group, width), narrow),
             pltpu.VMEM((8, group, width), narrow),
             pltpu.VMEM(spec, wide),
@@ -306,13 +399,25 @@
             pltpu.VMEM(part, narrow),
             pltpu.VMEM(part, wide),
             pltpu.VMEM((GROUP, nseq, width), wide),
+            pltpu.VMEM(blocks, narrow),
+            pltpu.VMEM((group, nseq * width // 8), wide),
             pltpu.SemaphoreType.DMA((8,)),
-            pltpu.SemaphoreType.DMA((8,)),
+            pltpu.SemaphoreType.DMA((9,)),
+            pltpu.SemaphoreType.DMA((4,)),
         ],
         compiler_params=pltpu.CompilerParams(
-            collective_id=0, has_side_effects=True, vmem_limit_bytes=48 * 2**20
+            collective_id=0, has_side_effects=True, vmem_limit_bytes=60 * 2**20
         ),
-    )(value, gated, taps.reshape(quarters), *tables)
+    )(grad_out, gate, value, taps.reshape(quarters), *tables)
+    return pl.pallas_call(
+        flush,
+        out_shape=shapes,
+        in_specs=[far] * 3,
+        out_specs=[far] * 3,
+        scratch_shapes=[pltpu.VMEM(shape.shape, shape.dtype) for shape in shapes]
+        + [pltpu.SemaphoreType.DMA((2, 12))],
+        compiler_params=pltpu.CompilerParams(vmem_limit_bytes=60 * 2**20),
+    )(*results)
 
 
 def on_device(grad_out, gate, value, filter_taps):
@@ -320,14 +425,12 @@
     ndp = lax.axis_size("dp")
     chans, width = grad_out.shape[1:]
     blocks = (nseq, chans // nseq, width)
-    gated = (grad_out[0].astype(jnp.float32) * gate[0].astype(jnp.float32)).astype(jnp.bfloat16)
     factor = 1.0 / (ndp * math.sqrt(nseq * width))
-    conv, grad_value, grad_filter = run_kernel(
-        value[0].reshape(blocks), gated.reshape(blocks), filter_taps.reshape(blocks), factor
+    grad_gate, grad_value, grad_filter = run_kernel(
+        *(array.reshape(blocks) for array in (grad_out, gate, value, filter_taps)), factor
     )
-    conv = conv.reshape(chans, width)
-    grad_gate = (grad_out[0].astype(jnp.float32) * conv.astype(jnp.float32)).astype(jnp.bfloat16)
-    return (grad_gate[None], grad_value.reshape(1, chans, width), grad_filter)
+    whole = (1, chans, width)
+    return (grad_gate.reshape(whole), grad_value.reshape(whole), grad_filter)
 
 
 def solution(mesh):

time: 125 us -> 122 us (0.976)
  other arithmetic: 2.36 us -> 0 us
  local copies, waits for them, and re-layouts: 1.52 us -> 0 us
    convert_element_type x2 -> x0, other arithmetic: 2.36 us -> none  [the longest x1 1.43 us: on_device(): (grad_out[0].astype(jnp.float32) * gate[0].astype(jnp.float32)).astype(jn...]
    pallas_call x0 -> x1, Pallas kernels: none -> 2.19 us  [run_kernel(): pl.pallas_call(flush, out_shape=shapes, in_specs=[far] * 3, out_specs=[fa...]
    pallas_call x1, Pallas kernels: 120 us -> 118 us  [run_kernel(): pl.pallas_call(functools.partial(kernel, factor), out_shape=shapes, in_sp...]
    unnamed x20 -> x0, local copies, waits for them, and re-layouts: 1.52 us -> none
where the time goes in v2:
time: 122 us; the launch traced here: 121 us
  Pallas kernels  120 us (98%)
    pallas_call x1, Pallas kernels, run_kernel(): pl.pallas_call(functools.partial(kernel, factor), out_shape=shapes, in_sp...  118 us

profile of v2, /device:TPU:1, one launch (start us, length us, event | category | flops | bytes accessed | tf_op | source)
XLA Modules:
  0.0 121.1 jit_solution(8298181232339045122)
XLA Ops:
  0.6 118.3 %shard_map.121 = (bf16[64,32,128]{2,1,0:T(8,128)(2,1)}, bf16[64,32,128]{2,1,0:T(8,128)(2,1)}, f32[32,1024]{1,0:T(8,128)}) custom-call(bf16[64,32,128]{2,1,0:T(8,128)(2,1)} %bitcast.6, bf16[64,32,128]{2,1,0:T(8,128)(2,1)} %bitcast.7, bf16[64,32,128]{2,1,0:T(8,128)(2,1)} %bitcast.8, bf16[8,4,2,32,128]{4,3,2,1,0:T(8,128)(2,1)} %bitcast.9, ...), custom_call_target="tpu_custom_call" | custom-call | tf_op jit(solution)/shard_map/pallas_call | solution.py:382
  118.9 2.2 %shard_map.122 = (bf16[64,32,128]{2,1,0:T(8,128)(2,1)}, bf16[64,32,128]{2,1,0:T(8,128)(2,1)}, f32[32,1024]{1,0:T(8,128)}) custom-call(bf16[64,32,128]{2,1,0:T(8,128)(2,1)} %get-tuple-element.9.refs_0_, bf16[64,32,128]{2,1,0:T(8,128)(2,1)} %get-tuple-element.10.refs_1_, f32[32,1024]{1,0:T(8,128)} %get-tuple-element.11.refs_2_), custom_call_target="tpu_custom_call" | custom-call | tf_op jit(solution)/shard_map/pallas_call | solution.py:412

commit v3 on v2

--- a/solution.py
+++ b/solution.py
@@ -12,7 +12,8 @@
 MESH = pl.DeviceIdType.MESH
 GROUP = 16
 EARLY = 40
-FIRST = 32
+FIRST = 46
+HALF = 40
 
 
 def make_tables(blocks, width, offset=0.25):
@@ -125,12 +126,12 @@
     gate,
     value,
     taps,
-    start,
-    forward,
-    backward,
-    finish,
-    twist_cos,
-    twist_sin,
+    start_far,
+    forward_far,
+    backward_far,
+    finish_far,
+    twist_cos_far,
+    twist_sin_far,
     grad_gate,
     grad_back,
     filter_grad,
@@ -156,6 +157,12 @@
     columns,
     gate_out,
     filter_out,
+    start,
+    forward,
+    backward,
+    finish,
+    twist_cos,
+    twist_sin,
     send_sem,
     recv_sem,
     load_sem,
@@ -205,7 +212,12 @@
         pltpu.make_async_copy(grad_out, grad_held, load_sem.at[0]),
         pltpu.make_async_copy(gate, gate_held, load_sem.at[1]),
     ]
-    for load in loads:
+    distant = (start_far, forward_far, backward_far, finish_far, twist_cos_far, twist_sin_far)
+    fetches = [
+        pltpu.make_async_copy(far, near, load_sem.at[4 + index])
+        for index, (far, near) in enumerate(zip(distant, tables))
+    ]
+    for load in loads + fetches:
         load.start()
     for load in loads:
         load.wait()
@@ -244,6 +256,8 @@
     take(value_cols.at[pl.ds(0, EARLY)], recv_sem.at[1])
     scatter(gated, gated_cols, send_sem.at[2], recv_sem.at[2], me, nseq)
 
+    for fetch in fetches:
+        fetch.wait()
     take(taps_cols.at[:, mine], recv_sem.at[0])
     for shift in range(1, 4):
         neighbour = lax.rem(plane + shift, 4) * 2 + half
@@ -281,7 +295,7 @@
         ).start()
     scatter(conv_send, conv_back, send_sem.at[4], recv_sem.at[4], me, nseq, FIRST)
     inverse_product(spec_taps, spec_gated, True, grad_send, mixed, partial, columns, tables)
-    scatter(grad_send, grad_back, send_sem.at[5], recv_sem.at[5], me, nseq, 0, FIRST)
+    scatter(grad_send, grad_back, send_sem.at[5], recv_sem.at[5], me, nseq, 0, HALF)
 
     take(y_recv, recv_sem.at[6])
 
@@ -300,7 +314,7 @@
         device_id_type=MESH,
     )
     swap.start()
-    scatter(grad_send, grad_back, send_sem.at[5], recv_sem.at[5], me, nseq, FIRST)
+    scatter(grad_send, grad_back, send_sem.at[5], recv_sem.at[5], me, nseq, HALF)
 
     take(conv_back, recv_sem.at[4])
     times(grad_held, conv_back, gate_out)
@@ -377,12 +391,11 @@
     quarters = (nseq // 8, 4, 2, group, width)
     spec = (group * nseq, 2 * width)
     part = (GROUP * nseq, 2 * width)
-    place = pl.BlockSpec(memory_space=pltpu.VMEM)
     far = pl.BlockSpec(memory_space=pl.ANY)
     results = pl.pallas_call(
         functools.partial(kernel, factor),
         out_shape=shapes,
-        in_specs=[far] * 4 + [place] * len(tables),
+        in_specs=[far] * (4 + len(tables)),
         out_specs=[far] * 3,
         scratch_shapes=[pltpu.VMEM(blocks, narrow) for _ in range(5)]
         + [pltpu.VMEM(quarters, narrow)]
@@ -401,9 +414,12 @@
             pltpu.VMEM((GROUP, nseq, width), wide),
             pltpu.VMEM(blocks, narrow),
             pltpu.VMEM((group, nseq * width // 8), wide),
+        ]
+        + [pltpu.VMEM(table.shape, table.dtype) for table in tables]
+        + [
             pltpu.SemaphoreType.DMA((8,)),
             pltpu.SemaphoreType.DMA((9,)),
-            pltpu.SemaphoreType.DMA((4,)),
+            pltpu.SemaphoreType.DMA((10,)),
         ],
         compiler_params=pltpu.CompilerParams(
             collective_id=0, has_side_effects=True, vmem_limit_bytes=60 * 2**20

time: 122 us -> 120 us (0.984)
  no operation moved by 1% of the time
where the time goes in v3:
time: 120 us
  Pallas kernels  119 us (99%)
    pallas_call x1, Pallas kernels, run_kernel(): pl.pallas_call(functools.partial(kernel, factor), out_shape=shapes, in_sp...  117 us

profile of v3, /device:TPU:1, one launch (start us, length us, event | category | flops | bytes accessed | tf_op | source)
XLA Modules:
  0.0 120.0 jit_solution(194845089841451082)
XLA Ops:
  0.6 117.2 %shard_map.121 = (bf16[64,32,128]{2,1,0:T(8,128)(2,1)}, bf16[64,32,128]{2,1,0:T(8,128)(2,1)}, f32[32,1024]{1,0:T(8,128)}) custom-call(bf16[64,32,128]{2,1,0:T(8,128)(2,1)} %bitcast.6, bf16[64,32,128]{2,1,0:T(8,128)(2,1)} %bitcast.7, bf16[64,32,128]{2,1,0:T(8,128)(2,1)} %bitcast.8, bf16[8,4,2,32,128]{4,3,2,1,0:T(8,128)(2,1)} %bitcast.9, ...), custom_call_target="tpu_custom_call" | custom-call | tf_op jit(solution)/shard_map/pallas_call | solution.py:395
  117.8 2.2 %shard_map.122 = (bf16[64,32,128]{2,1,0:T(8,128)(2,1)}, bf16[64,32,128]{2,1,0:T(8,128)(2,1)}, f32[32,1024]{1,0:T(8,128)}) custom-call(bf16[64,32,128]{2,1,0:T(8,128)(2,1)} %get-tuple-element.9.refs_0_, bf16[64,32,128]{2,1,0:T(8,128)(2,1)} %get-tuple-element.10.refs_1_, f32[32,1024]{1,0:T(8,128)} %get-tuple-element.11.refs_2_), custom_call_target="tpu_custom_call" | custom-call | tf_op jit(solution)/shard_map/pallas_call | solution.py:428

commit v4 on v3

--- a/solution.py
+++ b/solution.py
@@ -224,8 +224,6 @@
     times(grad_held, gate_held, gated)
     pl.semaphore_wait(barrier, nseq + 3 + nseq // 8)
 
-    scatter(value, value_cols, send_sem.at[1], recv_sem.at[1], me, nseq, 0, EARLY)
-    scatter(value, value_cols, send_sem.at[1], recv_sem.at[8], me, nseq, EARLY)
 
     def send_taps(step, carry):
         peer, row = taps_peer(step)
@@ -253,11 +251,7 @@
         return carry
 
     lax.fori_loop(0, nseq // 4, send_taps, 0)
-    take(value_cols.at[pl.ds(0, EARLY)], recv_sem.at[1])
-    scatter(gated, gated_cols, send_sem.at[2], recv_sem.at[2], me, nseq)
-
-    for fetch in fetches:
-        fetch.wait()
+    scatter(value, value_cols, send_sem.at[1], recv_sem.at[1], me, nseq, 0, EARLY)
     take(taps_cols.at[:, mine], recv_sem.at[0])
     for shift in range(1, 4):
         neighbour = lax.rem(plane + shift, 4) * 2 + half
@@ -269,6 +263,12 @@
             device_id={"dp": neighbour},
             device_id_type=MESH,
         ).start()
+    scatter(value, value_cols, send_sem.at[1], recv_sem.at[8], me, nseq, EARLY)
+    take(value_cols.at[pl.ds(0, EARLY)], recv_sem.at[1])
+    scatter(gated, gated_cols, send_sem.at[2], recv_sem.at[2], me, nseq)
+
+    for fetch in fetches:
+        fetch.wait()
     take(taps_cols.at[:, pl.ds(0, 3)], recv_sem.at[3])
     forward_spectrum(taps_cols.reshape(value.shape), spec_taps, mixed, tables)
 

time: 120 us -> 123 us (1.025); the launches traced: 120 us -> 121 us
  no operation moved by 1% of the time
where the time goes in v4:
time: 123 us; the launch traced here: 121 us
  Pallas kernels  120 us (98%)
    pallas_call x1, Pallas kernels, run_kernel(): pl.pallas_call(functools.partial(kernel, factor), out_shape=shapes, in_sp...  118 us

profile of v4, /device:TPU:1, one launch (start us, length us, event | category | flops | bytes accessed | tf_op | source)
XLA Modules:
  0.0 120.8 jit_solution(886035952674616471)
XLA Ops:
  0.6 117.9 %shard_map.121 = (bf16[64,32,128]{2,1,0:T(8,128)(2,1)}, bf16[64,32,128]{2,1,0:T(8,128)(2,1)}, f32[32,1024]{1,0:T(8,128)}) custom-call(bf16[64,32,128]{2,1,0:T(8,128)(2,1)} %bitcast.6, bf16[64,32,128]{2,1,0:T(8,128)(2,1)} %bitcast.7, bf16[64,32,128]{2,1,0:T(8,128)(2,1)} %bitcast.8, bf16[8,4,2,32,128]{4,3,2,1,0:T(8,128)(2,1)} %bitcast.9, ...), custom_call_target="tpu_custom_call" | custom-call | tf_op jit(solution)/shard_map/pallas_call | solution.py:395
  118.6 2.2 %shard_map.122 = (bf16[64,32,128]{2,1,0:T(8,128)(2,1)}, bf16[64,32,128]{2,1,0:T(8,128)(2,1)}, f32[32,1024]{1,0:T(8,128)}) custom-call(bf16[64,32,128]{2,1,0:T(8,128)(2,1)} %get-tuple-element.9.refs_0_, bf16[64,32,128]{2,1,0:T(8,128)(2,1)} %get-tuple-element.10.refs_1_, f32[32,1024]{1,0:T(8,128)} %get-tuple-element.11.refs_2_), custom_call_target="tpu_custom_call" | custom-call | tf_op jit(solution)/shard_map/pallas_call | solution.py:428
